TPU v7x, 32 devices: a whole 2x2x4 slice. The times are simulated.
32 devices in a mesh: row: 4 (over y, x), col: 2 (over core), dp: 4 (over z).
Axes of the slice: x: 2, y: 2, z: 4, core: 2. Of those that a mesh axis runs over, the one named last changes fastest.
Arguments:
- out_grad: bfloat16 [4, 128, 4096], P('dp', 'col', 'row'), may hold values from -6 to 6
- saved_hidden: bfloat16 [4, 128, 14336], P('dp', 'row', 'col'), may hold values from -6 to 6
- down_weight: bfloat16 [14336, 4096], P(('col', 'dp'), 'row'), may hold values from -0.046875 to 0.046875
Outputs:
- hidden_grad: bfloat16 [4, 128, 14336], P('dp', 'row', 'col')
- weight_grad: bfloat16 [14336, 4096], P(('col', 'dp'), 'row')
All inputs are finite; a program needn't handle non-finite values.
Results may differ from a plain program's by a relative error of at most 0.009.
Values may be sent and summed in bfloat16 or wider, within the bound.
A program may use at most 64 MiB of HBM per device.

v0:
```python
import jax
import jax.numpy as jnp
from jax import lax
from jax.sharding import PartitionSpec as P


def on_device(out_grad, saved_hidden, down_weight):
    grad_local = out_grad[0]
    hidden_local = saved_hidden[0]
    units = down_weight.shape[0]
    width = down_weight.shape[1]
    grad_replica = lax.all_gather(grad_local, "col", axis=0, tiled=True)
    grad_all = lax.all_gather(grad_replica[:, None, :], "dp", axis=1, tiled=True)
    tok_count = grad_all.shape[0]
    replica_count = grad_all.shape[1]
    local_tokens = hidden_local.shape[0]
    hidden_units = lax.all_to_all(
        hidden_local[:, None, :], "dp", split_axis=2, concat_axis=1, tiled=True
    )
    factor = jnp.float32(1.0) / jnp.sqrt(jnp.float32(tok_count * replica_count))
    flat_grad = grad_all.reshape(tok_count * replica_count, width)
    rows = flat_grad
    summed = lax.psum_scatter(
        lax.dot_general(
            rows, down_weight, (((1,), (1,)), ((), ())), preferred_element_type=jnp.float32
        ).astype(jnp.bfloat16),
        "row",
        scatter_dimension=0,
        tiled=True,
    )
    local_grad = summed.reshape(local_tokens, replica_count, units)
    returned = lax.all_to_all(local_grad, "dp", split_axis=1, concat_axis=2, tiled=True)
    hidden_grad = returned.reshape(1, local_tokens, -1)
    rows = grad_all
    left = lax.all_gather(hidden_units, "row", axis=0, tiled=True).reshape(-1, units)
    right = rows.reshape(-1, width)
    total = lax.dot_general(
        left, right, (((0,), (0,)), ((), ())), preferred_element_type=jnp.float32
    )
    weight_grad = (total * factor).astype(jnp.bfloat16)
    return (hidden_grad, weight_grad)


def solution(mesh):
    in_specs = (P("dp", "col", "row"), P("dp", "row", "col"), P(("col", "dp"), "row"))
    out_specs = (P("dp", "row", "col"), P(("col", "dp"), "row"))
    return jax.shard_map(
        on_device, mesh=mesh, in_specs=in_specs, out_specs=out_specs, check_vma=False
    )
```

profile of v0, /device:TPU:0, one launch (start us, length us, event | category | flops | bytes accessed | tf_op | source)
XLA Modules:
  0.0 169.9 jit_solution(11268376020256023476)
XLA Ops:
  7.2 0.0 all-gather.7.cloned.1.call-start
  7.2 2.3 %all-gather = bf16[1,128,1024]{2,1,0:T(8,128)(2,1)S(1)} all-gather(bf16[1,64,1024]{2,1,0:T(8,128)(2,1)} %param.3), channel_id=2, replica_groups=mesh['row'=4,'col'=2,'dp'=4] {'col'}, dimensions={1}, use_global_device_ids=true | all-gather | bytes 393216 | tf_op jit(solution)/shard_map/all_gather | solution.py:12
  9.5 0.8 copy.19
  10.4 0.0 all-gather.7.cloned.1.call-update
  10.4 0.0 reduce-scatter.2.cloned.1.call-start
  10.5 30.7 %all-gather.7.cloned.1.call-done = bf16[1,128,4096]{1,2,0:T(8,128)(2,1)} async-done(((bf16[1,128,1024]{1,2,0:T(8,128)(2,1)}), bf16[1,128,4096]{1,2,0:T(8,128)(2,1)}) %all-gather.7.cloned.1.call-update) | async-done | bytes 1048592 | tf_op jit(solution)/shard_map/all_gather | solution.py:13
  41.1 1.5 copy.20
  42.6 0.7 reshape.22
  43.3 0.0 copy-start.1
  43.3 5.4 %convolution_convert_fusion = bf16[512,1792]{1,0:T(8,128)(2,1)} fusion(bf16[512,1024]{1,0:T(8,128)(2,1)S(1)} %reshape.22, bf16[1792,1024]{1,0:T(8,128)(2,1)} %param.5), kind=kOutput, calls=%fused_computation.2 | convolution fusion | flops 1879965696 | bytes 6553600 | tf_op jit(solution)/shard_map/dot_general | solution.py:24
  48.8 0.0 reduce-scatter.2.cloned.1.call-update
  48.8 0.0 all-gather.5.cloned.1.call-start
  48.8 0.0 copy-done.1
  48.8 5.9 %copy.23 = bf16[32,1,7168]{0,1,2:T(2,128)(2,1)} copy(bf16[32,1,7168]{2,0,1:T(8,128)(2,1)S(1)} %bitcast.17) | data formatting | bytes 917504 | tf_op jit(solution)/shard_map/broadcast_in_dim;squeeze | solution.py:18
  54.8 0.5 broadcast
  55.3 39.8 %reduce = bf16[7168,32]{1,0:T(8,128)(2,1)S(1)} reduce(bf16[7168,1,32]{2,1,0:T(2,128)(2,1)} %bitcast.14, bf16[]{:T(256)} %broadcast), dimensions={1}, to_apply=%bitcast.8.reduce_sub_computation | reduce | bytes 917506
  95.1 1.8 %reshape.29 = bf16[4,2,28672]{2,1,0:T(2,128)(2,1)S(1)} reshape(bf16[7168,32]{1,0:T(8,128)(2,1)S(1)} %reduce) | data formatting | bytes 917504
  96.8 15.8 %all_to_all.21 = bf16[4,2,28672]{2,1,0:T(2,128)(2,1)S(1)} all-to-all(bf16[4,2,28672]{2,1,0:T(2,128)(2,1)S(1)} %reshape.29), channel_id=1, replica_groups=mesh['row'=4,'col'=2,'dp'=4] {'dp'}, dimensions={0} | all-to-all | bytes 917504 | tf_op jit(solution)/shard_map/all_to_all | solution.py:17
  112.7 3.0 %reshape.30 = bf16[7168,1,32]{2,1,0:T(2,128)(2,1)} reshape(bf16[4,2,28672]{2,1,0:T(2,128)(2,1)S(1)} %all_to_all.21) | data formatting | bytes 917504
  115.7 7.1 %copy.24 = bf16[32,1,7168]{2,0,1:T(8,128)(2,1)S(1)} copy(bf16[32,1,7168]{0,1,2:T(2,128)(2,1)} %bitcast.15) | data formatting | bytes 917504 | tf_op jit(solution)/shard_map/all_to_all | solution.py:17
  122.8 0.3 all_to_all.8
  123.1 0.8 copy.25
  123.9 0.0 all-gather.5.cloned.1.call-update
  123.9 0.0 reduce-scatter.2.cloned.1.call-done
  124.0 1.1 reshape.23
  125.1 0.8 copy.21
  125.9 3.6 %all-to-all-start = ((bf16[32,4,1792]{2,0,1:T(8,128)(2,1)}), bf16[32,4,1792]{2,0,1:T(8,128)(2,1)S(1)}, u32[]{:S(2)}, u32[]{:S(2)}) async-start(bf16[32,4,1792]{2,0,1:T(8,128)(2,1)} %copy.21), calls=%async_computation.1 | async-start | bytes 917504 | tf_op jit(solution)/shard_map/all_to_all | solution.py:32
  129.6 26.9 %all-gather.5.cloned.1.call-done = bf16[128,4,1792]{2,0,1:T(8,128)(2,1)} async-done(((bf16[32,4,1792]{2,0,1:T(8,128)(2,1)}), bf16[128,4,1792]{2,0,1:T(8,128)(2,1)}) %all-gather.5.cloned.1.call-update) | async-done | bytes 1835024 | tf_op jit(solution)/shard_map/all_gather | solution.py:35
  156.5 5.5 %fusion = bf16[1792,1024]{1,0:T(8,128)(2,1)} fusion(bf16[128,4,1792]{2,0,1:T(8,128)(2,1)} %all-gather.5.cloned.1.call-done, bf16[128,4,1024]{0,2,1:T(8,128)(2,1)S(1)} %bitcast.16), kind=kOutput, calls=%fused_computation.1 | convolution fusion | flops 1882718208 | bytes 6553600 | tf_op jit(solution)/shard_map/dot_general | solution.py:37
  161.9 0.0 all-to-all-done
  161.9 0.4 copy.22
  162.3 1.1 reshape.24
  (2 shorter events, 0.0 us)
Async XLA Ops:
  7.2 34.0 %all-gather.7.cloned.1.call-start = ((), (), s32[]{:S(2)}) async-start(), calls=%async_computation.5 | async-start | bytes 1310720 | tf_op jit(solution)/shard_map/all_gather | solution.py:13
  10.4 113.5 %reduce-scatter.2.cloned.1.call-start = ((), (), s32[]{:S(2)}) async-start(), calls=%async_computation.3 | async-start | bytes 2293760 | tf_op jit(solution)/shard_map/reduce_scatter | solution.py:23
  43.3 5.5 %copy-start.1 = (bf16[1,32,7168]{2,1,0:T(8,128)(2,1)S(1)}, bf16[1,32,7168]{2,1,0:T(8,128)(2,1)}, u32[]{:S(2)}) copy-start(bf16[1,32,7168]{2,1,0:T(8,128)(2,1)} %param.4) | copy-start | bytes 1376260
  48.8 107.7 %all-gather.5.cloned.1.call-start = ((), (), s32[]{:S(2)}) async-start(), calls=%async_computation.4 | async-start | bytes 2293760 | tf_op jit(solution)/shard_map/all_gather | solution.py:35
  115.7 40.8 %copy-start = (bf16[1,128,4096]{1,2,0:T(8,128)(2,1)S(1)}, bf16[1,128,4096]{1,2,0:T(8,128)(2,1)}, u32[]{:S(2)}) copy-start(bf16[1,128,4096]{1,2,0:T(8,128)(2,1)} %all-gather.7.cloned.1.call-done) | copy-start | bytes 3145732
  125.9 36.0 %all-to-all-start = ((bf16[32,4,1792]{2,0,1:T(8,128)(2,1)}), bf16[32,4,1792]{2,0,1:T(8,128)(2,1)S(1)}, u32[]{:S(2)}, u32[]{:S(2)}) async-start(bf16[32,4,1792]{2,0,1:T(8,128)(2,1)} %copy.21), calls=%async_computation.1 | async-start | bytes 917504 | tf_op jit(solution)/shard_map/all_to_all | solution.py:32
Sparse Core Ops, SparseCore 0:
  10.5 30.5 all-gather.6
  48.9 32.4 reduce-scatter.1
  124.1 32.3 all-gather.4
where the time goes:
time: 170 us
  waiting for transfers between devices  57.7 us (34%)
  other arithmetic  39.8 us (23%)
  local copies, waits for them, and re-layouts  25.9 us (15%)
  blocking collectives  18.2 us (11%)
  between operations  13.8 us (8%)
  matrix products  10.9 us (6%)
  starting transfers between devices  3.77 us (2%)
    unnamed x1, other arithmetic  39.8 us
    all_gather x1, waiting for transfers between devices, on_device(): lax.all_gather(grad_replica[:, None, :], 'dp', axis=1, tiled=True)  30.7 us
    all_gather x1, waiting for transfers between devices, on_device(): lax.all_gather(hidden_units, 'row', axis=0, tiled=True).reshape(-1, units)  26.9 us
    all_to_all x1, blocking collectives, on_device(): lax.all_to_all(hidden_local[:, None, :], 'dp', split_axis=2, concat_axis=...  15.8 us
    all_to_all x3, local copies, waits for them, and re-layouts, on_device(): lax.all_to_all(hidden_local[:, None, :], 'dp', split_axis=2, concat_axis=...  8.22 us
    another operation x1, local copies, waits for them, and re-layouts, on_device(): hidden_local[:, None, :]  5.94 us
    dot_general x1, matrix products, on_device(): lax.dot_general(left, right, (((0,), (0,)), ((), ())), preferred_element_...  5.47 us
    dot_general x1, matrix products, on_device(): lax.dot_general(rows, down_weight, (((1,), (1,)), ((), ())), preferred_el...  5.43 us
  transfers between devices with their start and end apart: 4, of which 2 were waited for; matrix products, arithmetic and copies ran while one was open for 39% of the time, Pallas kernels for 0%

commit v1 on v0

--- a/solution.py
+++ b/solution.py
@@ -1,10 +1,17 @@
+import functools
+
 import jax
 import jax.numpy as jnp
+import numpy as np
 from jax import lax
+from jax.experimental import pallas as pl
+from jax.experimental.pallas import tpu as pltpu
 from jax.sharding import PartitionSpec as P
 
-
-def on_device(out_grad, saved_hidden, down_weight):
+MESH = pl.DeviceIdType.MESH
+
+
+def by_collectives(out_grad, saved_hidden, down_weight):
     grad_local = out_grad[0]
     hidden_local = saved_hidden[0]
     units = down_weight.shape[0]
@@ -41,7 +48,220 @@
     return (hidden_grad, weight_grad)
 
 
+def kernel(
+    n_dp, n_row, factor,
+    g, h, w, hg, wg,
+    gfull, hfull, wv, part, rs, hsum, acc, wbuf,
+    loc_sem, zg_s, zg_r, zh_s, zh_r, cg_s, cg_r, ag_s, ag_r, rs_s, rs_r, hz_s, hz_r, wo_sem,
+):
+    row = lax.axis_index("row")
+    col = lax.axis_index("col")
+    dp = lax.axis_index("dp")
+    units, width = w.shape
+    toks = h.shape[0]
+    half = toks // 2
+    tile = 256 if units % 256 == 0 else 128
+    tiles = units // tile
+
+    def dev(r=None, c=None, z=None):
+        return {"row": row if r is None else r, "col": col if c is None else c,
+                "dp": dp if z is None else z}
+
+    def send(src, dst, ssem, rsem, to):
+        cp = pltpu.make_async_remote_copy(
+            src_ref=src, dst_ref=dst, send_sem=ssem, recv_sem=rsem,
+            device_id=to, device_id_type=MESH)
+        cp.start()
+        return cp
+
+    barrier = pltpu.get_barrier_semaphore()
+    peers = [dev(c=1 - col)]
+    peers += [dev(z=dp ^ k) for k in range(1, n_dp)]
+    peers += [dev(r=row ^ j) for j in range(1, n_row)]
+    for p in peers:
+        pl.semaphore_signal(barrier, inc=1, device_id=p, device_id_type=MESH)
+
+    def columns(z):
+        return pl.ds(pl.multiple_of(z * units, 128), units)
+
+    load_w = pltpu.make_async_copy(w, wv, loc_sem.at[0])
+    load_g = pltpu.make_async_copy(g, gfull.at[0, col], loc_sem.at[1])
+    load_h = pltpu.make_async_copy(h.at[:, columns(dp)], hfull.at[0, row], loc_sem.at[2])
+    load_g.start()
+    load_w.start()
+    load_h.start()
+    pl.semaphore_wait(barrier, len(peers))
+
+    zg, zh, cg, agx, agy, fwx, fwy, hz = {}, {}, {}, {}, {}, {}, {}, {}
+    rsc = {}
+    cg[0] = send(g, gfull.at[0, col], cg_s.at[0], cg_r.at[0], dev(c=1 - col))
+    for k in range(1, n_dp):
+        zg[k] = send(g, gfull.at[k, col], zg_s.at[k], zg_r.at[k], dev(z=dp ^ k))
+
+    def gather_own(k):
+        src = h.at[:, columns(dp)] if k == 0 else hfull.at[k, row]
+        agx[k] = send(src, hfull.at[k, row], ag_s.at[k, 0], ag_r.at[k, 0], dev(r=row ^ 1))
+        agy[k] = send(src, hfull.at[k, row], ag_s.at[k, 1], ag_r.at[k, 1], dev(r=row ^ 2))
+
+    def forward(k):
+        agx[k].wait_recv()
+        a = hfull.at[k, row ^ 1, pl.ds(0, half)]
+        fwy[k] = send(a, a, ag_s.at[k, 2], ag_r.at[k, 2], dev(r=row ^ 2))
+        agy[k].wait_recv()
+        b = hfull.at[k, row ^ 2, pl.ds(half, half)]
+        fwx[k] = send(b, b, ag_s.at[k, 3], ag_r.at[k, 3], dev(r=row ^ 1))
+
+    gather_own(0)
+    for k in range(1, n_dp):
+        zh[k] = send(h.at[:, columns(dp ^ k)], hfull.at[k, row], zh_s.at[k], zh_r.at[k],
+                     dev(z=dp ^ k))
+
+    def partner(k):
+        zg[k].wait_recv()
+        src = gfull.at[k, col]
+        cg[k] = send(src, src, cg_s.at[k], cg_r.at[k], dev(c=1 - col))
+
+    def hidden_partial(j):
+        lhs = gfull[2 * j:2 * j + 2].reshape(-1, width)
+
+        @pl.loop(0, tiles)
+        def _(i):
+            at = pl.ds(pl.multiple_of(i * tile, tile), tile)
+            res = lax.dot_general(lhs, wv[at, :], (((1,), (1,)), ((), ())),
+                                  preferred_element_type=jnp.float32)
+            part[2 * j:2 * j + 2, :, :, at] = res.astype(jnp.bfloat16).reshape(
+                2, n_row, toks, tile)
+
+        for k in (2 * j, 2 * j + 1):
+            for q in range(1, n_row):
+                rsc[k, q] = send(part.at[k, row ^ q], rs.at[k, q - 1], rs_s.at[k, q],
+                                 rs_r.at[k, q], dev(r=row ^ q))
+
+    def finish_hidden(k):
+        for q in range(1, n_row):
+            rsc[k, q].wait_recv()
+        s = part[k, row].astype(jnp.float32)
+        for q in range(1, n_row):
+            s = s + rs[k, q - 1].astype(jnp.float32)
+        hsum[k] = s.astype(jnp.bfloat16)
+        dst = hg.at[:, columns(dp)]
+        if k == 0:
+            hz[0] = pltpu.make_async_copy(hsum.at[0], dst, loc_sem.at[3])
+            hz[0].start()
+        else:
+            hz[k] = send(hsum.at[k], dst, hz_s.at[k], hz_r.at[k], dev(z=dp ^ k))
+
+    def weight_part(j, first, last):
+        for k in (2 * j, 2 * j + 1):
+            fwx[k].wait_recv()
+            fwy[k].wait_recv()
+        rhs = gfull[2 * j:2 * j + 2].reshape(-1, width)
+
+        @pl.loop(0, tiles)
+        def _(i):
+            at = pl.ds(pl.multiple_of(i * tile, tile), tile)
+            lhs = hfull[2 * j:2 * j + 2, :, :, at].reshape(-1, tile)
+            res = lax.dot_general(lhs, rhs, (((0,), (0,)), ((), ())),
+                                  preferred_element_type=jnp.float32)
+            if not first:
+                res = acc[at, :] + res
+            if last:
+                wbuf[at, :] = (res * factor).astype(jnp.bfloat16)
+                pltpu.make_async_copy(wbuf.at[at], wg.at[at], wo_sem.at[i]).start()
+            else:
+                acc[at, :] = res
+
+    pairs = n_dp // 2
+    load_w.wait()
+    load_g.wait()
+    load_h.wait()
+    partner(1)
+    cg[0].wait_recv()
+    cg[1].wait_recv()
+    hidden_partial(0)
+    forward(0)
+    zh[1].wait_recv()
+    gather_own(1)
+    for j in range(1, pairs):
+        for k in (2 * j, 2 * j + 1):
+            partner(k)
+        for k in (2 * j, 2 * j + 1):
+            cg[k].wait_recv()
+        hidden_partial(j)
+        forward(2 * j - 1)
+        for k in (2 * j, 2 * j + 1):
+            zh[k].wait_recv()
+            gather_own(k)
+        finish_hidden(2 * j - 1)
+        finish_hidden(2 * j - 2)
+        weight_part(j - 1, j == 1, False)
+        forward(2 * j)
+    forward(n_dp - 1)
+    finish_hidden(n_dp - 1)
+    finish_hidden(n_dp - 2)
+    weight_part(pairs - 1, pairs == 1, True)
+
+    for k in range(1, n_dp):
+        hz[k].wait()
+        zg[k].wait_send()
+        zh[k].wait_send()
+    hz[0].wait()
+    for k in range(n_dp):
+        for cp in (cg[k], agx[k], agy[k], fwx[k], fwy[k]):
+            cp.wait_send()
+        for q in range(1, n_row):
+            rsc[k, q].wait_send()
+
+    @pl.loop(0, tiles)
+    def _(i):
+        at = pl.ds(pl.multiple_of(i * tile, tile), tile)
+        pltpu.make_async_copy(wbuf.at[at], wg.at[at], wo_sem.at[i]).wait()
+
+
+def by_kernel(n_dp, n_row, out_grad, saved_hidden, down_weight):
+    g, h, w = out_grad[0], saved_hidden[0], down_weight
+    units, width = w.shape
+    gt, toks = g.shape[0], h.shape[0]
+    bf = jnp.bfloat16
+    factor = np.float32(1.0) / np.sqrt(np.float32(n_dp * n_row * toks))
+    dma = pltpu.SemaphoreType.DMA
+    hg, wg = pl.pallas_call(
+        functools.partial(kernel, n_dp, n_row, factor),
+        out_shape=(jax.ShapeDtypeStruct(h.shape, bf), jax.ShapeDtypeStruct(w.shape, bf)),
+        in_specs=[pl.BlockSpec(memory_space=pl.ANY)] * 3,
+        out_specs=[pl.BlockSpec(memory_space=pl.ANY)] * 2,
+        scratch_shapes=[
+            pltpu.VMEM((n_dp, 2, gt, width), bf),
+            pltpu.VMEM((n_dp, n_row, toks, units), bf),
+            pltpu.VMEM((units, width), bf),
+            pltpu.VMEM((n_dp, n_row, toks, units), bf),
+            pltpu.VMEM((n_dp, n_row - 1, toks, units), bf),
+            pltpu.VMEM((n_dp, toks, units), bf),
+            pltpu.VMEM((units, width), jnp.float32),
+            pltpu.VMEM((units, width), bf),
+            dma((4,)), dma((n_dp,)), dma((n_dp,)), dma((n_dp,)), dma((n_dp,)),
+            dma((n_dp,)), dma((n_dp,)), dma((n_dp, 4)), dma((n_dp, 4)),
+            dma((n_dp, n_row)), dma((n_dp, n_row)), dma((n_dp,)), dma((n_dp,)),
+            dma((units // 128,)),
+        ],
+        compiler_params=pltpu.CompilerParams(
+            collective_id=0, has_side_effects=True, vmem_limit_bytes=48 * 1024 * 1024),
+    )(g, h, w)
+    return hg[None], wg
+
+
 def solution(mesh):
+    n_row, n_col, n_dp = mesh.shape["row"], mesh.shape["col"], mesh.shape["dp"]
+
+    def on_device(out_grad, saved_hidden, down_weight):
+        units = down_weight.shape[0]
+        toks = saved_hidden.shape[1]
+        fits = (n_row == 4 and n_col == 2 and n_dp in (2, 4, 8) and units % 128 == 0
+                and toks % 32 == 0 and out_grad.shape[1] % 16 == 0)
+        if not fits:
+            return by_collectives(out_grad, saved_hidden, down_weight)
+        return by_kernel(n_dp, n_row, out_grad, saved_hidden, down_weight)
+
     in_specs = (P("dp", "col", "row"), P("dp", "row", "col"), P(("col", "dp"), "row"))
     out_specs = (P("dp", "row", "col"), P(("col", "dp"), "row"))
     return jax.shard_map(

time: 170 us -> 63.9 us (0.38)
  Pallas kernels: 0 us -> 58.6 us
  waiting for transfers between devices: 57.7 us -> 0 us
  other arithmetic: 39.8 us -> 0 us
  local copies, waits for them, and re-layouts: 25.9 us -> 4.52 us
  blocking collectives: 18.2 us -> 0 us
  between operations: 13.8 us -> 0.65 us
  matrix products: 10.9 us -> 0 us
  starting transfers between devices: 3.77 us -> 0 us
    pallas_call x0 -> x1, Pallas kernels: none -> 58.6 us  [by_kernel(): pl.pallas_call(functools.partial(kernel, n_dp, n_row, factor), out_shape=...]
    all_gather x2 -> x0, waiting for transfers between devices: 57.6 us -> none  [the longest x1 30.7 us: on_device(): lax.all_gather(grad_replica[:, None, :], 'dp', axis=1, tiled=True)]
    unnamed x1 -> x0, other arithmetic: 39.8 us -> none
    all_to_all x1 -> x0, blocking collectives: 15.8 us -> none  [on_device(): lax.all_to_all(hidden_local[:, None, :], 'dp', split_axis=2, concat_axis=...]
    dot_general x2 -> x0, matrix products: 10.9 us -> none  [the longest x1 5.47 us: on_device(): lax.dot_general(left, right, (((0,), (0,)), ((), ())), preferred_element_...]
    all_to_all x4 -> x0, local copies, waits for them, and re-layouts: 8.57 us -> none  [the longest x3 8.22 us: on_device(): lax.all_to_all(hidden_local[:, None, :], 'dp', split_axis=2, concat_axis=...]
    another operation x1 -> x0, local copies, waits for them, and re-layouts: 5.94 us -> none  [on_device(): hidden_local[:, None, :]]
    reshape x4 -> x0, local copies, waits for them, and re-layouts: 3.73 us -> none  [the longest x2 1.94 us: on_device(): local_grad = summed.reshape(local_tokens, replica_count, units)]
  transfers between devices with their start and end apart: 4 -> 0, of which waited for: 2 -> 0; matrix products, arithmetic and copies ran while one was open for 39% -> 0% of each run, Pallas kernels for 0% -> 0%
where the time goes in v1:
time: 63.9 us; the launch traced here: 63.8 us
  Pallas kernels  58.6 us (92%)
  local copies, waits for them, and re-layouts  4.52 us (7%)
  between operations  0.65 us (1%)
    pallas_call x1, Pallas kernels, by_kernel(): pl.pallas_call(functools.partial(kernel, n_dp, n_row, factor), out_shape=...  58.6 us
    unnamed x6, local copies, waits for them, and re-layouts  4.52 us

profile of v1, /device:TPU:0, one launch (start us, length us, event | category | flops | bytes accessed | tf_op | source)
XLA Modules:
  0.0 63.8 jit_solution(8238866930406693408)
XLA Ops:
  0.6 0.0 copy-start
  0.6 1.0 %copy-done = bf16[1,32,7168]{2,1,0:T(8,128)(2,1)S(1)} copy-done((bf16[1,32,7168]{2,1,0:T(8,128)(2,1)S(1)}, bf16[1,32,7168]{2,1,0:T(8,128)(2,1)}, u32[]{:S(2)}) %copy-start) | copy-done | bytes 458776
  1.6 0.0 copy-start.1
  1.7 0.9 %copy-done.1 = bf16[1,64,1024]{2,1,0:T(8,128)(2,1)S(1)} copy-done((bf16[1,64,1024]{2,1,0:T(8,128)(2,1)S(1)}, bf16[1,64,1024]{2,1,0:T(8,128)(2,1)}, u32[]{:S(2)}) %copy-start.1) | copy-done | bytes 131096
  2.6 58.6 %shard_map.50 = (bf16[32,7168]{1,0:T(8,128)(2,1)S(1)}, bf16[1792,1024]{1,0:T(8,128)(2,1)S(1)}) custom-call(bf16[64,1024]{1,0:T(8,128)(2,1)S(1)} %bitcast.5, bf16[32,7168]{1,0:T(8,128)(2,1)S(1)} %bitcast.3, bf16[1792,1024]{1,0:T(8,128)(2,1)} %w.1), custom_call_target="tpu_custom_call" | custom-call | tf_op jit(solution)/shard_map/pallas_call | solution.py:228
  61.2 0.8 %copy.7 = bf16[1,32,7168]{2,1,0:T(8,128)(2,1)} copy(bf16[1,32,7168]{2,1,0:T(8,128)(2,1)S(1)} %bitcast.4) | data formatting | bytes 917504
  61.9 1.8 %copy.8 = bf16[1792,1024]{1,0:T(8,128)(2,1)} copy(bf16[1792,1024]{1,0:T(8,128)(2,1)S(1)} %get-tuple-element.9) | data formatting | bytes 7340032
Async XLA Ops:
  0.6 1.0 %copy-start = (bf16[1,32,7168]{2,1,0:T(8,128)(2,1)S(1)}, bf16[1,32,7168]{2,1,0:T(8,128)(2,1)}, u32[]{:S(2)}) copy-start(bf16[1,32,7168]{2,1,0:T(8,128)(2,1)} %param.4) | copy-start | bytes 1376260
  1.6 0.9 %copy-start.1 = (bf16[1,64,1024]{2,1,0:T(8,128)(2,1)S(1)}, bf16[1,64,1024]{2,1,0:T(8,128)(2,1)}, u32[]{:S(2)}) copy-start(bf16[1,64,1024]{2,1,0:T(8,128)(2,1)} %param.3) | copy-start | bytes 393220

commit v2 on v1

v2 whole, which is shorter than its diff:
```python
import functools

import jax
import jax.numpy as jnp
import numpy as np
from jax import lax
from jax.experimental import pallas as pl
from jax.experimental.pallas import tpu as pltpu
from jax.sharding import PartitionSpec as P

MESH = pl.DeviceIdType.MESH


def by_collectives(out_grad, saved_hidden, down_weight):
    grad_local = out_grad[0]
    hidden_local = saved_hidden[0]
    units = down_weight.shape[0]
    width = down_weight.shape[1]
    grad_replica = lax.all_gather(grad_local, "col", axis=0, tiled=True)
    grad_all = lax.all_gather(grad_replica[:, None, :], "dp", axis=1, tiled=True)
    tok_count = grad_all.shape[0]
    replica_count = grad_all.shape[1]
    local_tokens = hidden_local.shape[0]
    hidden_units = lax.all_to_all(
        hidden_local[:, None, :], "dp", split_axis=2, concat_axis=1, tiled=True
    )
    factor = jnp.float32(1.0) / jnp.sqrt(jnp.float32(tok_count * replica_count))
    flat_grad = grad_all.reshape(tok_count * replica_count, width)
    rows = flat_grad
    summed = lax.psum_scatter(
        lax.dot_general(
            rows, down_weight, (((1,), (1,)), ((), ())), preferred_element_type=jnp.float32
        ).astype(jnp.bfloat16),
        "row",
        scatter_dimension=0,
        tiled=True,
    )
    local_grad = summed.reshape(local_tokens, replica_count, units)
    returned = lax.all_to_all(local_grad, "dp", split_axis=1, concat_axis=2, tiled=True)
    hidden_grad = returned.reshape(1, local_tokens, -1)
    rows = grad_all
    left = lax.all_gather(hidden_units, "row", axis=0, tiled=True).reshape(-1, units)
    right = rows.reshape(-1, width)
    total = lax.dot_general(
        left, right, (((0,), (0,)), ((), ())), preferred_element_type=jnp.float32
    )
    weight_grad = (total * factor).astype(jnp.bfloat16)
    return (hidden_grad, weight_grad)


def kernel(
    n_dp, n_row, factor,
    g, h, w, hg, wg,
    gfull, hfull, wv, part, rx, ry, mid_out, mid_in, hsum, acc, wbuf,
    loc_sem, zg_s, zg_r, zf_s, zh_s, zh_r, cg_s, cg_r, ag_s, ag_r, rs_s, rs_r, hz_s, hz_r, wo_sem,
):
    row = lax.axis_index("row")
    col = lax.axis_index("col")
    dp = lax.axis_index("dp")
    ry_i, rx_i = row // 2, row % 2
    inner = jnp.logical_or(dp == 1, dp == 2)
    outer = jnp.logical_not(inner)
    units, width = w.shape
    toks = h.shape[0]
    half = toks // 2
    tile = 256 if units % 256 == 0 else 128
    tiles = units // tile

    def dev(r=None, c=None, z=None):
        return {"row": row if r is None else r, "col": col if c is None else c,
                "dp": dp if z is None else z}

    xn, yn, pn = dev(r=row ^ 1), dev(r=row ^ 2), dev(c=1 - col)

    def remote(src, dst, ssem, rsem, to):
        return pltpu.make_async_remote_copy(
            src_ref=src, dst_ref=dst, send_sem=ssem, recv_sem=rsem,
            device_id=to, device_id_type=MESH)

    def send(*args):
        cp = remote(*args)
        cp.start()
        return cp

    def columns(z):
        return pl.ds(pl.multiple_of(z * units, 128), units)

    barrier = pltpu.get_barrier_semaphore()
    peers = [pn] + [dev(z=dp ^ k) for k in range(1, n_dp)] + [xn, yn]
    for p in peers:
        pl.semaphore_signal(barrier, inc=1, device_id=p, device_id_type=MESH)
    load_g = pltpu.make_async_copy(g, gfull.at[0, col], loc_sem.at[1])
    load_w = pltpu.make_async_copy(w, wv, loc_sem.at[0])
    load_h = pltpu.make_async_copy(h.at[:, columns(dp)], hfull.at[0, row], loc_sem.at[2])
    load_g.start()
    load_w.start()
    load_h.start()
    pl.semaphore_wait(barrier, len(peers))

    agx, agy, fwx, fwy, hz = {}, {}, {}, {}, {}
    r1 = {}

    def grad_to(k):
        return remote(g, gfull.at[k, col], zg_s.at[k], zg_r.at[k], dev(z=dp ^ k))

    def grad_on(k_here, k_there, step):
        return remote(gfull.at[k_here, col], gfull.at[k_there, col], zf_s.at[k_here],
                      zg_r.at[k_there], dev(z=dp ^ step))

    def grad_pair(k):
        src = gfull.at[k, col]
        return remote(src, src, cg_s.at[k], cg_r.at[k], pn)

    def hidden_to(k):
        return remote(h.at[:, columns(dp ^ k)], hfull.at[k, row], zh_s.at[k], zh_r.at[k],
                      dev(z=dp ^ k))

    grad_to(1).start()

    @pl.when(inner)
    def _():
        grad_to(3).start()

    cg0 = send(g, gfull.at[0, col], cg_s.at[0], cg_r.at[0], pn)

    def gather_own(k):
        src = h.at[:, columns(dp)] if k == 0 else hfull.at[k, row]
        agx[k] = send(src, hfull.at[k, row], ag_s.at[k, 0], ag_r.at[k, 0], xn)
        agy[k] = send(src, hfull.at[k, row], ag_s.at[k, 1], ag_r.at[k, 1], yn)

    def forward(k):
        agx[k].wait_recv()
        a = hfull.at[k, row ^ 1, pl.ds(0, half)]
        fwy[k] = send(a, a, ag_s.at[k, 2], ag_r.at[k, 2], yn)
        agy[k].wait_recv()
        b = hfull.at[k, row ^ 2, pl.ds(half, half)]
        fwx[k] = send(b, b, ag_s.at[k, 3], ag_r.at[k, 3], xn)

    gather_own(0)

    def hidden_partial(lo, hi):
        lhs = gfull[lo:hi].reshape(-1, width)

        @pl.loop(0, tiles)
        def _(i):
            at = pl.ds(pl.multiple_of(i * tile, tile), tile)
            res = lax.dot_general(lhs, wv[at, :], (((1,), (1,)), ((), ())),
                                  preferred_element_type=jnp.float32)
            part[lo:hi, :, :, :, :, at] = res.astype(jnp.bfloat16).reshape(
                hi - lo, 2, 2, 2, half, tile)

        for k in range(lo, hi):
            r1[k, 0] = send(part.at[k, :, rx_i ^ 1, 0], rx.at[k], rs_s.at[k, 0],
                            rs_r.at[k, 0], xn)
            r1[k, 1] = send(part.at[k, ry_i ^ 1, :, 1], ry.at[k], rs_s.at[k, 1],
                            rs_r.at[k, 1], yn)

    f32, bf16 = jnp.float32, jnp.bfloat16

    def red_first(k):
        return remote(mid_out.at[k, 0], mid_in.at[k, 0], rs_s.at[k, 2], rs_r.at[k, 2], yn)

    def red_second(k):
        return remote(mid_out.at[k, 1], mid_in.at[k, 1], rs_s.at[k, 3], rs_r.at[k, 3], xn)

    def reduce_on(k):
        r1[k, 0].wait_recv()
        mid_out[k, 0] = (part[k, ry_i ^ 1, rx_i, 0].astype(f32)
                         + rx[k, ry_i ^ 1].astype(f32)).astype(bf16)
        red_first(k).start()
        r1[k, 1].wait_recv()
        mid_out[k, 1] = (part[k, ry_i, rx_i ^ 1, 1].astype(f32)
                         + ry[k, rx_i ^ 1].astype(f32)).astype(bf16)
        red_second(k).start()

    def finish_hidden(k):
        red_first(k).wait_recv()
        hsum[k, 0:half] = (part[k, ry_i, rx_i, 0].astype(f32) + rx[k, ry_i].astype(f32)
                           + mid_in[k, 0].astype(f32)).astype(bf16)
        red_second(k).wait_recv()
        hsum[k, half:toks] = (part[k, ry_i, rx_i, 1].astype(f32) + ry[k, rx_i].astype(f32)
                              + mid_in[k, 1].astype(f32)).astype(bf16)
        dst = hg.at[:, columns(dp)]
        if k == 0:
            hz[0] = pltpu.make_async_copy(hsum.at[0], dst, loc_sem.at[3])
            hz[0].start()
        else:
            hz[k] = send(hsum.at[k], dst, hz_s.at[k], hz_r.at[k], dev(z=dp ^ k))

    def weight_part(lo, hi, first, last):
        for k in range(lo, hi):
            fwx[k].wait_recv()
            fwy[k].wait_recv()
        rhs = gfull[lo:hi].reshape(-1, width)

        @pl.loop(0, tiles)
        def _(i):
            at = pl.ds(pl.multiple_of(i * tile, tile), tile)
            lhs = hfull[lo:hi, :, :, at].reshape(-1, tile)
            res = lax.dot_general(lhs, rhs, (((0,), (0,)), ((), ())),
                                  preferred_element_type=f32)
            if not first:
                res = acc[at, :] + res
            if last:
                wbuf[at, :] = (res * factor).astype(bf16)
                pltpu.make_async_copy(wbuf.at[at], wg.at[at], wo_sem.at[i]).start()
            else:
                acc[at, :] = res

    load_g.wait()
    grad_to(1).wait_recv()
    grad_pair(1).start()

    @pl.when(inner)
    def _():
        grad_on(1, 2, 3).start()
        grad_to(3).wait_recv()
        grad_on(3, 2, 1).start()
        grad_pair(3).start()

    load_h.wait()
    forward(0)

    @pl.when(inner)
    def _():
        grad_to(2).wait_recv()
        grad_on(2, 3, 1).start()
        grad_pair(2).start()
        for k in (3, 2, 1):
            hidden_to(k).start()

    load_w.wait()
    cg0.wait_recv()
    grad_pair(1).wait_recv()
    hidden_partial(0, 2)

    @pl.when(outer)
    def _():
        grad_to(2).wait_recv()
        grad_pair(2).start()
        for k in (1, 2, 3):
            hidden_to(k).start()

    grad_pair(2).wait_recv()
    hidden_partial(2, 3)

    @pl.when(outer)
    def _():
        reduce_on(0)
        grad_to(3).wait_recv()
        grad_pair(3).start()
        reduce_on(1)

    grad_pair(3).wait_recv()
    hidden_partial(3, 4)
    hidden_to(1).wait_recv()
    gather_own(1)
    weight_part(0, 1, True, False)
    reduce_on(2)
    reduce_on(3)
    for k in (2, 3):
        hidden_to(k).wait_recv()
        gather_own(k)
    forward(1)
    finish_hidden(2)
    finish_hidden(3)

    @pl.when(inner)
    def _():
        reduce_on(1)
        reduce_on(0)

    forward(2)
    forward(3)
    weight_part(1, 2, False, False)
    finish_hidden(1)
    finish_hidden(0)
    weight_part(2, 4, False, True)

    @pl.when(inner)
    def _():
        grad_to(3).wait_send()
        grad_on(1, 2, 3).wait_send()
        grad_on(3, 2, 1).wait_send()
        grad_on(2, 3, 1).wait_send()

    grad_to(1).wait_send()
    cg0.wait_send()
    hz[0].wait()
    for k in range(n_dp):
        if k:
            hz[k].wait()
            hidden_to(k).wait_send()
            grad_pair(k).wait_send()
        for cp in (agx[k], agy[k], fwx[k], fwy[k], r1[k, 0], r1[k, 1], red_first(k), red_second(k)):
            cp.wait_send()

    @pl.loop(0, tiles)
    def _(i):
        at = pl.ds(pl.multiple_of(i * tile, tile), tile)
        pltpu.make_async_copy(wbuf.at[at], wg.at[at], wo_sem.at[i]).wait()


def by_kernel(n_dp, n_row, out_grad, saved_hidden, down_weight):
    g, h, w = out_grad[0], saved_hidden[0], down_weight
    units, width = w.shape
    gt, toks = g.shape[0], h.shape[0]
    bf = jnp.bfloat16
    factor = np.float32(1.0) / np.sqrt(np.float32(n_dp * n_row * toks))
    dma = pltpu.SemaphoreType.DMA
    hg, wg = pl.pallas_call(
        functools.partial(kernel, n_dp, n_row, factor),
        out_shape=(jax.ShapeDtypeStruct(h.shape, bf), jax.ShapeDtypeStruct(w.shape, bf)),
        in_specs=[pl.BlockSpec(memory_space=pl.ANY)] * 3,
        out_specs=[pl.BlockSpec(memory_space=pl.ANY)] * 2,
        scratch_shapes=[
            pltpu.VMEM((n_dp, 2, gt, width), bf),
            pltpu.VMEM((n_dp, n_row, toks, units), bf),
            pltpu.VMEM((units, width), bf),
            pltpu.VMEM((n_dp, 2, 2, 2, toks // 2, units), bf),
            pltpu.VMEM((n_dp, 2, toks // 2, units), bf),
            pltpu.VMEM((n_dp, 2, toks // 2, units), bf),
            pltpu.VMEM((n_dp, 2, toks // 2, units), bf),
            pltpu.VMEM((n_dp, 2, toks // 2, units), bf),
            pltpu.VMEM((n_dp, toks, units), bf),
            pltpu.VMEM((units, width), jnp.float32),
            pltpu.VMEM((units, width), bf),
            dma((4,)), dma((n_dp,)), dma((n_dp,)), dma((n_dp,)), dma((n_dp,)), dma((n_dp,)),
            dma((n_dp,)), dma((n_dp,)), dma((n_dp, 4)), dma((n_dp, 4)),
            dma((n_dp, 4)), dma((n_dp, 4)), dma((n_dp,)), dma((n_dp,)),
            dma((units // 128,)),
        ],
        compiler_params=pltpu.CompilerParams(
            collective_id=0, has_side_effects=True, vmem_limit_bytes=62 * 1024 * 1024),
    )(g, h, w)
    return hg[None], wg


def solution(mesh):
    n_row, n_col, n_dp = mesh.shape["row"], mesh.shape["col"], mesh.shape["dp"]

    def on_device(out_grad, saved_hidden, down_weight):
        units = down_weight.shape[0]
        toks = saved_hidden.shape[1]
        fits = (n_row == 4 and n_col == 2 and n_dp == 4 and units % 128 == 0
                and toks % 32 == 0 and out_grad.shape[1] % 16 == 0)
        if not fits:
            return by_collectives(out_grad, saved_hidden, down_weight)
        return by_kernel(n_dp, n_row, out_grad, saved_hidden, down_weight)

    in_specs = (P("dp", "col", "row"), P("dp", "row", "col"), P(("col", "dp"), "row"))
    out_specs = (P("dp", "row", "col"), P(("col", "dp"), "row"))
    return jax.shard_map(
        on_device, mesh=mesh, in_specs=in_specs, out_specs=out_specs, check_vma=False
    )
```

time: 63.9 us -> 53.3 us (0.83)
  Pallas kernels: 58.6 us -> 46.4 us
  local copies, waits for them, and re-layouts: 4.52 us -> 6.06 us
    pallas_call x1, Pallas kernels: 58.6 us -> 46.4 us  [by_kernel(): pl.pallas_call(functools.partial(kernel, n_dp, n_row, factor), out_shape=...]
    unnamed x6 -> x2, local copies, waits for them, and re-layouts: 4.52 us -> 6.06 us
where the time goes in v2:
time: 53.3 us; the launch traced here: 53.1 us
  Pallas kernels  46.4 us (87%)
  local copies, waits for them, and re-layouts  6.06 us (11%)
  between operations  0.64 us (1%)
    pallas_call x1, Pallas kernels, by_kernel(): pl.pallas_call(functools.partial(kernel, n_dp, n_row, factor), out_shape=...  46.4 us
    unnamed x2, local copies, waits for them, and re-layouts  6.06 us

profile of v2, /device:TPU:0, one launch (start us, length us, event | category | flops | bytes accessed | tf_op | source)
XLA Modules:
  0.0 53.1 jit_solution(3055232383925708076)
XLA Ops:
  0.6 46.4 %shard_map.50 = (bf16[32,7168]{1,0:T(8,128)(2,1)}, bf16[1792,1024]{1,0:T(8,128)(2,1)}) custom-call(bf16[64,1024]{1,0:T(8,128)(2,1)} %bitcast.5, bf16[32,7168]{1,0:T(8,128)(2,1)} %bitcast.3, bf16[1792,1024]{1,0:T(8,128)(2,1)} %w.1), custom_call_target="tpu_custom_call" | custom-call | tf_op jit(solution)/shard_map/pallas_call | solution.py:311
  47.0 1.8 %copy.7 = bf16[1,32,7168]{2,1,0:T(8,128)(2,1)} copy(bf16[1,32,7168]{2,1,0:T(8,128)(2,1)} %bitcast.4) | data formatting | bytes 917504
  48.8 4.2 %copy.8 = bf16[1792,1024]{1,0:T(8,128)(2,1)} copy(bf16[1792,1024]{1,0:T(8,128)(2,1)} %get-tuple-element.9) | data formatting | bytes 7340032

commit v3 on v2

--- a/solution.py
+++ b/solution.py
@@ -51,8 +51,8 @@
 def kernel(
     n_dp, n_row, factor,
     g, h, w, hg, wg,
-    gfull, hfull, wv, part, rx, ry, mid_out, mid_in, hsum, acc, wbuf,
-    loc_sem, zg_s, zg_r, zf_s, zh_s, zh_r, cg_s, cg_r, ag_s, ag_r, rs_s, rs_r, hz_s, hz_r, wo_sem,
+    gfull, hfull, wv, part, rx, ry, mid_out, mid_in, hsum, acc,
+    loc_sem, zg_s, zg_r, zf_s, zh_s, zh_r, cg_s, cg_r, ag_s, ag_r, rs_s, rs_r, hz_s, hz_r,
 ):
     row = lax.axis_index("row")
     col = lax.axis_index("col")
@@ -97,7 +97,7 @@
     load_h.start()
     pl.semaphore_wait(barrier, len(peers))
 
-    agx, agy, fwx, fwy, hz = {}, {}, {}, {}, {}
+    agx, agy, fwx, fwy = {}, {}, {}, {}
     r1 = {}
 
     def grad_to(k):
@@ -173,6 +173,12 @@
                          + ry[k, rx_i ^ 1].astype(f32)).astype(bf16)
         red_second(k).start()
 
+    def back_to(k):
+        dst = hg.at[:, columns(dp)]
+        if k == 0:
+            return pltpu.make_async_copy(hsum.at[0], dst, loc_sem.at[3])
+        return remote(hsum.at[k], dst, hz_s.at[k], hz_r.at[k], dev(z=dp ^ k))
+
     def finish_hidden(k):
         red_first(k).wait_recv()
         hsum[k, 0:half] = (part[k, ry_i, rx_i, 0].astype(f32) + rx[k, ry_i].astype(f32)
@@ -180,12 +186,7 @@
         red_second(k).wait_recv()
         hsum[k, half:toks] = (part[k, ry_i, rx_i, 1].astype(f32) + ry[k, rx_i].astype(f32)
                               + mid_in[k, 1].astype(f32)).astype(bf16)
-        dst = hg.at[:, columns(dp)]
-        if k == 0:
-            hz[0] = pltpu.make_async_copy(hsum.at[0], dst, loc_sem.at[3])
-            hz[0].start()
-        else:
-            hz[k] = send(hsum.at[k], dst, hz_s.at[k], hz_r.at[k], dev(z=dp ^ k))
+        back_to(k).start()
 
     def weight_part(lo, hi, first, last):
         for k in range(lo, hi):
@@ -202,8 +203,7 @@
             if not first:
                 res = acc[at, :] + res
             if last:
-                wbuf[at, :] = (res * factor).astype(bf16)
-                pltpu.make_async_copy(wbuf.at[at], wg.at[at], wo_sem.at[i]).start()
+                wg[at, :] = (res * factor).astype(bf16)
             else:
                 acc[at, :] = res
 
@@ -253,28 +253,27 @@
 
     grad_pair(3).wait_recv()
     hidden_partial(3, 4)
+    @pl.when(inner)
+    def _():
+        reduce_on(0)
+        reduce_on(1)
+
+    weight_part(0, 1, True, False)
+    reduce_on(2)
     hidden_to(1).wait_recv()
     gather_own(1)
-    weight_part(0, 1, True, False)
-    reduce_on(2)
     reduce_on(3)
     for k in (2, 3):
         hidden_to(k).wait_recv()
         gather_own(k)
+    finish_hidden(1)
+    finish_hidden(2)
     forward(1)
-    finish_hidden(2)
     finish_hidden(3)
-
-    @pl.when(inner)
-    def _():
-        reduce_on(1)
-        reduce_on(0)
-
+    finish_hidden(0)
     forward(2)
     forward(3)
     weight_part(1, 2, False, False)
-    finish_hidden(1)
-    finish_hidden(0)
     weight_part(2, 4, False, True)
 
     @pl.when(inner)
@@ -286,23 +285,18 @@
 
     grad_to(1).wait_send()
     cg0.wait_send()
-    hz[0].wait()
+    back_to(0).wait()
     for k in range(n_dp):
         if k:
-            hz[k].wait()
+            back_to(k).wait()
             hidden_to(k).wait_send()
             grad_pair(k).wait_send()
         for cp in (agx[k], agy[k], fwx[k], fwy[k], r1[k, 0], r1[k, 1], red_first(k), red_second(k)):
             cp.wait_send()
 
-    @pl.loop(0, tiles)
-    def _(i):
-        at = pl.ds(pl.multiple_of(i * tile, tile), tile)
-        pltpu.make_async_copy(wbuf.at[at], wg.at[at], wo_sem.at[i]).wait()
-
 
 def by_kernel(n_dp, n_row, out_grad, saved_hidden, down_weight):
-    g, h, w = out_grad[0], saved_hidden[0], down_weight
+    g, h, w = (pltpu.with_memory_space_constraint(a, pltpu.HBM) for a in (out_grad[0], saved_hidden[0], down_weight))
     units, width = w.shape
     gt, toks = g.shape[0], h.shape[0]
     bf = jnp.bfloat16
@@ -311,8 +305,8 @@
     hg, wg = pl.pallas_call(
         functools.partial(kernel, n_dp, n_row, factor),
         out_shape=(jax.ShapeDtypeStruct(h.shape, bf), jax.ShapeDtypeStruct(w.shape, bf)),
-        in_specs=[pl.BlockSpec(memory_space=pl.ANY)] * 3,
-        out_specs=[pl.BlockSpec(memory_space=pl.ANY)] * 2,
+        in_specs=[pl.BlockSpec(memory_space=pltpu.HBM)] * 3,
+        out_specs=[pl.BlockSpec(memory_space=pl.ANY), pl.BlockSpec(memory_space=pltpu.VMEM)],
         scratch_shapes=[
             pltpu.VMEM((n_dp, 2, gt, width), bf),
             pltpu.VMEM((n_dp, n_row, toks, units), bf),
@@ -324,14 +318,12 @@
             pltpu.VMEM((n_dp, 2, toks // 2, units), bf),
             pltpu.VMEM((n_dp, toks, units), bf),
             pltpu.VMEM((units, width), jnp.float32),
-            pltpu.VMEM((units, width), bf),
             dma((4,)), dma((n_dp,)), dma((n_dp,)), dma((n_dp,)), dma((n_dp,)), dma((n_dp,)),
             dma((n_dp,)), dma((n_dp,)), dma((n_dp, 4)), dma((n_dp, 4)),
             dma((n_dp, 4)), dma((n_dp, 4)), dma((n_dp,)), dma((n_dp,)),
-            dma((units // 128,)),
         ],
         compiler_params=pltpu.CompilerParams(
-            collective_id=0, has_side_effects=True, vmem_limit_bytes=62 * 1024 * 1024),
+            collective_id=0, has_side_effects=True, vmem_limit_bytes=44 * 1024 * 1024),
     )(g, h, w)
     return hg[None], wg
 

time: 53.3 us -> 48.5 us (0.910); the launches traced: 53.1 us -> 47.6 us
  local copies, waits for them, and re-layouts: 6.06 us -> 2.61 us
  Pallas kernels: 46.4 us -> 44.4 us
    unnamed x2, local copies, waits for them, and re-layouts: 6.06 us -> 2.61 us
    pallas_call x1, Pallas kernels: 46.4 us -> 44.4 us  [by_kernel(): pl.pallas_call(functools.partial(kernel, n_dp, n_row, factor), out_shape=...]
where the time goes in v3:
time: 48.5 us; the launch traced here: 47.6 us
  Pallas kernels  44.4 us (92%)
  local copies, waits for them, and re-layouts  2.61 us (5%)
  between operations  0.64 us (1%)
    pallas_call x1, Pallas kernels, by_kernel(): pl.pallas_call(functools.partial(kernel, n_dp, n_row, factor), out_shape=...  44.4 us
    unnamed x2, local copies, waits for them, and re-layouts  2.61 us

profile of v3, /device:TPU:0, one launch (start us, length us, event | category | flops | bytes accessed | tf_op | source)
XLA Modules:
  0.0 47.6 jit_solution(16231101751722511795)
XLA Ops:
  0.6 44.4 %shard_map.50 = (bf16[32,7168]{1,0:T(8,128)(2,1)S(1)}, bf16[1792,1024]{1,0:T(8,128)(2,1)S(1)}) custom-call(bf16[64,1024]{1,0:T(8,128)(2,1)} %bitcast.5, bf16[32,7168]{1,0:T(8,128)(2,1)} %bitcast.4, bf16[1792,1024]{1,0:T(8,128)(2,1)} %w.1), custom_call_target="tpu_custom_call" | custom-call | tf_op jit(solution)/shard_map/pallas_call | solution.py:305
  45.0 0.8 %copy.7 = bf16[1,32,7168]{2,1,0:T(8,128)(2,1)} copy(bf16[1,32,7168]{2,1,0:T(8,128)(2,1)S(1)} %bitcast.3) | data formatting | bytes 917504
  45.8 1.8 %copy.8 = bf16[1792,1024]{1,0:T(8,128)(2,1)} copy(bf16[1792,1024]{1,0:T(8,128)(2,1)S(1)} %get-tuple-element.9) | data formatting | bytes 7340032

commit v4 on v3

--- a/solution.py
+++ b/solution.py
@@ -208,6 +208,9 @@
                 acc[at, :] = res
 
     load_g.wait()
+    load_w.wait()
+    cg0.wait_recv()
+    hidden_partial(0, 1)
     grad_to(1).wait_recv()
     grad_pair(1).start()
 
@@ -229,10 +232,8 @@
         for k in (3, 2, 1):
             hidden_to(k).start()
 
-    load_w.wait()
-    cg0.wait_recv()
     grad_pair(1).wait_recv()
-    hidden_partial(0, 2)
+    hidden_partial(1, 2)
 
     @pl.when(outer)
     def _():
@@ -252,6 +253,8 @@
         reduce_on(1)
 
     grad_pair(3).wait_recv()
+    hidden_to(1).wait_recv()
+    gather_own(1)
     hidden_partial(3, 4)
     @pl.when(inner)
     def _():
@@ -260,8 +263,6 @@
 
     weight_part(0, 1, True, False)
     reduce_on(2)
-    hidden_to(1).wait_recv()
-    gather_own(1)
     reduce_on(3)
     for k in (2, 3):
         hidden_to(k).wait_recv()

time: 48.5 us -> 48.5 us (level); the launches traced: 47.6 us -> 48.3 us
  Pallas kernels: 44.4 us -> 45.1 us
    pallas_call x1, Pallas kernels: 44.4 us -> 45.1 us  [by_kernel(): pl.pallas_call(functools.partial(kernel, n_dp, n_row, factor), out_shape=...]
where the time goes in v4:
time: 48.5 us; the launch traced here: 48.3 us
  Pallas kernels  45.1 us (93%)
  local copies, waits for them, and re-layouts  2.61 us (5%)
  between operations  0.64 us (1%)
    pallas_call x1, Pallas kernels, by_kernel(): pl.pallas_call(functools.partial(kernel, n_dp, n_row, factor), out_shape=...  45.1 us
    unnamed x2, local copies, waits for them, and re-layouts  2.61 us

profile of v4, /device:TPU:0, one launch (start us, length us, event | category | flops | bytes accessed | tf_op | source)
XLA Modules:
  0.0 48.3 jit_solution(13099045783907508243)
XLA Ops:
  0.6 45.1 %shard_map.50 = (bf16[32,7168]{1,0:T(8,128)(2,1)S(1)}, bf16[1792,1024]{1,0:T(8,128)(2,1)S(1)}) custom-call(bf16[64,1024]{1,0:T(8,128)(2,1)} %bitcast.5, bf16[32,7168]{1,0:T(8,128)(2,1)} %bitcast.4, bf16[1792,1024]{1,0:T(8,128)(2,1)} %w.1), custom_call_target="tpu_custom_call" | custom-call | tf_op jit(solution)/shard_map/pallas_call | solution.py:306
  45.7 0.8 %copy.7 = bf16[1,32,7168]{2,1,0:T(8,128)(2,1)} copy(bf16[1,32,7168]{2,1,0:T(8,128)(2,1)S(1)} %bitcast.3) | data formatting | bytes 917504
  46.5 1.8 %copy.8 = bf16[1792,1024]{1,0:T(8,128)(2,1)} copy(bf16[1792,1024]{1,0:T(8,128)(2,1)S(1)} %get-tuple-element.9) | data formatting | bytes 7340032
